TPU v7x, 32 devices: a whole 2x2x4 slice. The times are simulated.
32 devices in a mesh: bond: 8 (over z, x), mpo: 4 (over y, core).
Axes of the slice: x: 2, y: 2, z: 4, core: 2. Of those that a mesh axis runs over, the one named last changes fastest.
Arguments:
- wave_blocks: bfloat16 [8, 16, 256, 256], P('bond'), may hold values from -6 to 6
- left_environment: bfloat16 [8, 8, 256, 256], P('mpo', 'bond'), may hold values from -0.375 to 0.375
- right_environment: bfloat16 [8, 8, 256, 256], P('mpo', 'bond'), may hold values from -0.375 to 0.375
- site_operators: bfloat16 [8, 16, 16], P('mpo'), may hold values from -1.1953125 to 1.1953125
- right_sector: int32 [8, 16, 1], P('bond'), may hold values from 0 to 7; in each aligned block of 16 rows (0 to 15, 16 to 31, ..., all dimensions but the last counted through in order) at most 2 rows name the same one
- left_sizes: int32 [8], replicated, may hold values from 128 to 256
- right_sizes: int32 [8], replicated, may hold values from 128 to 256
- sector_place: int32 [8], replicated, may hold values from 0 to 7, each once
Outputs:
- applied: bfloat16 [8, 16, 256, 256], P('bond', 'mpo')
Inputs may be any that keep to these rules, and one draw needn't show every extreme that they name: `right_sector`: among the 16 blocks of one bond index no right sector is named more than 2 times, a bound that some block reaches. `sector_place`: every position is taken by exactly one right sector.
All inputs are finite; a program needn't handle non-finite values.
Results may differ from a plain program's by a relative error of at most 0.0057.
Values may be sent and summed in bfloat16 or wider, within the bound.
A program may use at most 64 MiB of HBM per device.

v0:
```python
import jax
import jax.numpy as jnp
from jax import lax
from jax.sharding import PartitionSpec as P


def lookup(entries, indices):
    count = entries.shape[0]
    matches = indices[..., None] == jnp.arange(count, dtype=jnp.int32)
    return jnp.sum(jnp.where(matches, entries, 0), axis=-1)


def shards(
    wave_blocks,
    left_environment,
    right_environment,
    site_operators,
    right_sector,
    left_sizes,
    right_sizes,
    sector_place,
):
    sectors = wave_blocks.shape[0]
    states = wave_blocks.shape[1]
    block_rows = wave_blocks.shape[2]
    channels = left_environment.shape[0]
    first_sector = lax.axis_index("bond") * sectors
    sector_ids = right_sector[:, :, 0]
    offsets = jnp.arange(block_rows, dtype=jnp.int32)
    left_live = lax.dynamic_slice_in_dim(left_sizes, first_sector, sectors)
    row_mask = offsets[None, :] < left_live[:, None]
    column_mask = offsets[None, None, :] < lookup(right_sizes, sector_ids)[:, :, None]
    live_mask = row_mask[:, None, :, None] & column_mask[:, :, None, :]
    masked = jnp.where(live_mask, wave_blocks, jnp.zeros((), jnp.bfloat16))
    block_count = sectors * states
    flat_blocks = masked.reshape(block_count, block_rows, block_rows)
    place_flat = lookup(sector_place, sector_ids).reshape(block_count)
    gathered = lax.all_gather(right_environment, "bond", axis=1, tiled=True)
    chosen = jnp.take(gathered, place_flat, axis=1)
    right_part = jnp.einsum(
        "bac,hbxc->bhax", flat_blocks, chosen, preferred_element_type=jnp.float32
    ).astype(jnp.bfloat16)
    right_part = right_part.reshape(sectors, states, channels, block_rows, block_rows)
    same_sector = sector_ids[:, :, None] == sector_ids[:, None, :]
    mixing = jnp.where(same_sector[:, None], site_operators[None], jnp.zeros((), jnp.bfloat16))
    mixed = jnp.einsum(
        "nhst,nthac->nshac", mixing, right_part, preferred_element_type=jnp.float32
    ).astype(jnp.bfloat16)
    partial_value = jnp.einsum(
        "hnab,nshbc->nsac", left_environment, mixed, preferred_element_type=jnp.float32
    )
    per_device = states // lax.axis_size("mpo")
    first_state = lax.axis_index("mpo") * per_device
    summed = lax.psum(partial_value, "mpo")
    summed = lax.dynamic_slice_in_dim(summed, first_state, per_device, 1)
    kept_mask = lax.dynamic_slice_in_dim(live_mask, first_state, per_device, 1)
    return jnp.where(kept_mask, summed, jnp.zeros((), jnp.float32)).astype(jnp.bfloat16)


def solution(mesh):
    placed = (
        P("bond", None, None, None),
        P("mpo", "bond", None, None),
        P("mpo", "bond", None, None),
        P("mpo", None, None),
        P("bond", None, None),
        P(),
        P(),
        P(),
    )
    return jax.shard_map(
        shards, mesh=mesh, in_specs=placed, out_specs=P("bond", "mpo", None, None), check_vma=False
    )
```

profile of v0, /device:TPU:0, one launch (start us, length us, event | category | flops | bytes accessed | tf_op | source)
XLA Modules:
  0.0 172.7 jit_solution(5104987714782508854)
XLA Ops:
  6.5 0.0 copy-start
  6.5 0.0 copy-start.5
  6.5 0.0 copy-start.2
  6.5 0.0 copy-start.3
  6.5 0.0 copy-start.4
  6.5 0.0 all-gather.2.cloned.1.call-start
  6.6 0.7 all-gather.2.cloned.1.call-update
  7.3 2.9 %copy.12 = bf16[1,16,256,256]{2,3,1,0:T(8,128)(2,1)S(1)} copy(bf16[1,16,256,256]{3,2,1,0:T(8,128)(2,1)} %param.8) | data formatting | bytes 4194304 | tf_op args[0]
  10.2 0.0 copy-done.5
  10.2 0.6 dynamic_slice.9
  10.8 0.6 iota_compare_fusion.2
  11.4 0.0 copy-done.2
  11.4 0.0 copy-done.3
  11.4 0.0 copy-done.4
  11.4 0.1 select_reduce_fusion.1
  11.6 0.1 broadcast_compare_fusion
  11.6 0.1 iota_compare_fusion
  11.7 2.0 %broadcast_and_fusion = pred[1,16,256,256]{2,3,1,0:T(8,128)(4,1)} fusion(pred[16,256]{1,0:T(8,128)(4,1)S(1)} %iota_compare_fusion, pred[256]{0:T(512)(128)(4,1)S(1)} %iota_compare_fusion.2), kind=kLoop, calls=%fused_computation.15 | loop fusion | flops 1048576 | bytes 1052928 | tf_op jit(solution)/shard_map/and | solution.py:33
  13.7 47.6 %all-gather.2.cloned.1.call-done = bf16[2,8,256,256]{3,2,1,0:T(8,128)(2,1)} async-done(((bf16[2,1,256,256]{3,2,1,0:T(8,128)(2,1)}), bf16[2,8,256,256]{3,2,1,0:T(8,128)(2,1)}) %all-gather.2.cloned.1.call-update) | async-done | bytes 2097168 | tf_op jit(solution)/shard_map/all_gather | solution.py:38
  61.4 4.3 %gather_fusion = bf16[16,2,256,256]{3,2,1,0:T(8,128)(2,1)} fusion(bf16[2,8,256,256]{3,2,1,0:T(8,128)(2,1)} %all-gather.2.cloned.1.call-done, s32[1024]{0:T(1024)S(1)} %pad_clamp_fusion), kind=kCustom, calls=%fused_computation | custom fusion | bytes 8388672 | tf_op jit(solution)/shard_map/jit(_take)/gather | solution.py:39
  65.7 4.7 %fusion.2 = bf16[16,2,256,256]{3,2,1,0:T(8,128)(2,1)} fusion(bf16[16,2,256,256]{3,2,1,0:T(8,128)(2,1)} %gather_fusion, pred[16]{0:T(512)(128)(4,1)S(1)} %compare_and_fusion, bf16[1,16,256,256]{2,3,1,0:T(8,128)(2,1)S(1)} %copy.12, pred[16,256]{1,0:T(8,128)(4,1)S(1)} %iota_compare_fusion, pred[256]{0:T(512)(128)(4,1)S(1)} %iota_compare_fusion.2), kind=kOutput, calls=%fused_computation.3 | convolution fusion | flops 1077936128 | bytes 10490128 | tf_op jit(solution)/shard_map/bac,hbxc->bhax/dot_general | solution.py:40
  70.4 0.0 copy-start.1
  70.4 7.9 %copy.16 = bf16[16,2,256,256]{2,0,3,1:T(8,128)(2,1)} copy(bf16[16,2,256,256]{3,2,1,0:T(8,128)(2,1)} %fusion.2) | data formatting | bytes 8388608 | tf_op jit(solution)/shard_map/bac,hbxc->bhax/dot_general | solution.py:40
  78.3 0.0 copy-done.1
  78.3 3.4 %convert_bitcast_fusion = bf16[16,2,256,256]{3,0,2,1:T(8,128)(2,1)S(1)} fusion(bf16[16,2,256,256]{2,0,3,1:T(8,128)(2,1)} %copy.16, bf16[2,16,16]{2,1,0:T(8,128)(2,1)S(1)} %copy-done.1, pred[16,16]{1,0:T(8,128)(4,1)S(1)} %broadcast_compare_fusion), kind=kOutput, calls=%fused_computation.8 | convolution fusion | flops 69206528 | bytes 8389888 | tf_op jit(solution)/shard_map/nhst,nthac->nshac/dot_general | solution.py:46
  81.7 0.0 copy-done
  81.7 6.1 %fusion.11 = f32[1,16,256,256]{2,3,1,0:T(8,128)} fusion(bf16[16,2,256,256]{3,0,2,1:T(8,128)(2,1)S(1)} %convert_bitcast_fusion, bf16[2,1,256,256]{3,2,1,0:T(8,128)(2,1)S(1)} %copy-done), kind=kOutput, calls=%fused_computation.11 | convolution fusion | flops 1073741824 | bytes 8650752 | tf_op jit(solution)/shard_map/hnab,nshbc->nsac/dot_general | solution.py:49
  87.8 75.9 %all-reduce.1 = bf16[1,16,256,256]{2,3,1,0:T(8,128)(2,1)S(1)} all-reduce(f32[1,16,256,256]{2,3,1,0:T(8,128)} %fusion.11), channel_id=1, replica_groups=mesh['bond'=8,'mpo'=4] {'mpo'}, use_global_device_ids=true, to_apply=%region_2.3 | all-reduce | flops 1048576 | bytes 6291456 | tf_op jit(solution)/shard_map/psum | solution.py:54
  163.7 1.1 select_convert_fusion
  164.8 1.0 copy.14
  (3 shorter events, 0.0 us)
Async XLA Ops:
  6.5 75.1 %copy-start = (bf16[2,1,256,256]{3,2,1,0:T(8,128)(2,1)S(1)}, bf16[2,1,256,256]{3,2,1,0:T(8,128)(2,1)}, u32[]{:S(2)}) copy-start(bf16[2,1,256,256]{3,2,1,0:T(8,128)(2,1)} %param.9) | copy-start | bytes 786436
  6.5 3.6 %copy-start.5 = (s32[8]{0:T(128)S(1)}, s32[8]{0:T(128)}, u32[]{:S(2)}) copy-start(s32[8]{0:T(128)} %param.13) | copy-start | bytes 100
  6.5 4.9 %copy-start.2 = (s32[1,16,1]{1,2,0:T(1,128)S(1)}, s32[1,16,1]{1,2,0:T(1,128)}, u32[]{:S(2)}) copy-start(s32[1,16,1]{1,2,0:T(1,128)} %param.12) | copy-start | bytes 196
  6.5 4.9 %copy-start.3 = (s32[8]{0:T(128)S(1)}, s32[8]{0:T(128)}, u32[]{:S(2)}) copy-start(s32[8]{0:T(128)} %param.14) | copy-start | bytes 100
  6.5 4.9 %copy-start.4 = (s32[8]{0:T(128)S(1)}, s32[8]{0:T(128)}, u32[]{:S(2)}) copy-start(s32[8]{0:T(128)} %param.15) | copy-start | bytes 100
  6.5 54.8 %all-gather.2.cloned.1.call-start = ((), (), s32[]{:S(2)}) async-start(), calls=%async_computation | async-start | bytes 2359296 | tf_op jit(solution)/shard_map/all_gather | solution.py:38
  70.4 7.9 %copy-start.1 = (bf16[2,16,16]{2,1,0:T(8,128)(2,1)S(1)}, bf16[2,16,16]{2,1,0:T(8,128)(2,1)}, u32[]{:S(2)}) copy-start(bf16[2,16,16]{2,1,0:T(8,128)(2,1)} %param.11) | copy-start | bytes 3076
Sparse Core Ops, SparseCore 0:
  9.5 51.7 all-gather.1
where the time goes:
time: 173 us
  blocking collectives  75.9 us (44%)
  waiting for transfers between devices  48.3 us (28%)
  local copies, waits for them, and re-layouts  16.7 us (10%)
  matrix products  14.2 us (8%)
  between operations  13.5 us (8%)
  other arithmetic  4.04 us (2%)
    psum x1, blocking collectives, shards(): summed = lax.psum(partial_value, 'mpo')  75.9 us
    all_gather x1, waiting for transfers between devices, shards(): gathered = lax.all_gather(right_environment, 'bond', axis=1, tiled=True)  47.6 us
    dot_general x1, local copies, waits for them, and re-layouts, shards(): jnp.einsum('bac,hbxc->bhax', flat_blocks, chosen, preferred_element_type=...  7.89 us
    dot_general x1, matrix products, shards(): jnp.einsum('hnab,nshbc->nsac', left_environment, mixed, preferred_element...  6.13 us
    dot_general x1, matrix products, shards(): jnp.einsum('bac,hbxc->bhax', flat_blocks, chosen, preferred_element_type=...  4.66 us
    gather x1, local copies, waits for them, and re-layouts, shards(): chosen = jnp.take(gathered, place_flat, axis=1)  4.34 us
  transfers between devices with their start and end apart: 1, of which 1 were waited for; matrix products, arithmetic and copies ran while one was open for 4% of the time, Pallas kernels for 0%

commit v1 on v0

--- a/solution.py
+++ b/solution.py
@@ -51,7 +51,8 @@
     )
     per_device = states // lax.axis_size("mpo")
     first_state = lax.axis_index("mpo") * per_device
-    summed = lax.psum(partial_value, "mpo")
+    blocks = lax.all_gather(partial_value, "mpo", axis=0, tiled=False)
+    summed = blocks.sum(axis=0)
     summed = lax.dynamic_slice_in_dim(summed, first_state, per_device, 1)
     kept_mask = lax.dynamic_slice_in_dim(live_mask, first_state, per_device, 1)
     return jnp.where(kept_mask, summed, jnp.zeros((), jnp.float32)).astype(jnp.bfloat16)

time: 173 us -> 214 us (1.24)
  waiting for transfers between devices: 48.3 us -> 155 us
  blocking collectives: 75.9 us -> 0 us
  other arithmetic: 4.04 us -> 11.4 us
    all_gather x0 -> x1, waiting for transfers between devices: none -> 104 us  [shards(): blocks = lax.all_gather(partial_value, 'mpo', axis=0, tiled=False)]
    psum x1 -> x0, blocking collectives: 75.9 us -> none  [shards(): summed = lax.psum(partial_value, 'mpo')]
    dot_general x1 -> x0, local copies, waits for them, and re-layouts: 7.89 us -> none  [shards(): jnp.einsum('bac,hbxc->bhax', flat_blocks, chosen, preferred_element_type=...]
    reduce_sum x0 -> x1, other arithmetic: none -> 7.51 us  [shards(): summed = blocks.sum(axis=0)]
    convert_element_type x1, local copies, waits for them, and re-layouts: 1 us -> 7.89 us  [shards(): right_part = jnp.einsum('bac,hbxc->bhax', flat_blocks, chosen, preferred_...]
    transpose x0 -> x1, local copies, waits for them, and re-layouts: none -> 5.35 us  [shards(): jnp.einsum('hnab,nshbc->nsac', left_environment, mixed, preferred_element...]
    unnamed x13 -> x6, local copies, waits for them, and re-layouts: 2.88 us -> 0.01 us
    all_gather x1, waiting for transfers between devices: 47.6 us -> 50.4 us  [shards(): gathered = lax.all_gather(right_environment, 'bond', axis=1, tiled=True)]
  transfers between devices with their start and end apart: 1 -> 2, of which waited for: 1 -> 2; matrix products, arithmetic and copies ran while one was open for 4% -> 2% of each run, Pallas kernels for 0% -> 0%
where the time goes in v1:
time: 214 us
  waiting for transfers between devices  155 us (72%)
  local copies, waits for them, and re-layouts  18.8 us (9%)
  matrix products  15.1 us (7%)
  between operations  13.5 us (6%)
  other arithmetic  11.4 us (5%)
    all_gather x1, waiting for transfers between devices, shards(): blocks = lax.all_gather(partial_value, 'mpo', axis=0, tiled=False)  104 us
    all_gather x1, waiting for transfers between devices, shards(): gathered = lax.all_gather(right_environment, 'bond', axis=1, tiled=True)  50.4 us
    convert_element_type x1, local copies, waits for them, and re-layouts, shards(): right_part = jnp.einsum('bac,hbxc->bhax', flat_blocks, chosen, preferred_...  7.89 us
    reduce_sum x1, other arithmetic, shards(): summed = blocks.sum(axis=0)  7.51 us
    dot_general x1, matrix products, shards(): jnp.einsum('hnab,nshbc->nsac', left_environment, mixed, preferred_element...  6.13 us
    dot_general x1, matrix products, shards(): jnp.einsum('bac,hbxc->bhax', flat_blocks, chosen, preferred_element_type=...  5.54 us
    transpose x1, local copies, waits for them, and re-layouts, shards(): jnp.einsum('hnab,nshbc->nsac', left_environment, mixed, preferred_element...  5.35 us
    gather x1, local copies, waits for them, and re-layouts, shards(): chosen = jnp.take(gathered, place_flat, axis=1)  4.34 us
  transfers between devices with their start and end apart: 2, of which 2 were waited for; matrix products, arithmetic and copies ran while one was open for 2% of the time, Pallas kernels for 0%

profile of v1, /device:TPU:0, one launch (start us, length us, event | category | flops | bytes accessed | tf_op | source)
XLA Modules:
  0.0 214.0 jit_solution(14440453127684700390)
XLA Ops:
  6.5 0.0 copy-start
  6.5 0.0 all-gather.4.cloned.1.call-start
  6.5 0.7 all-gather.4.cloned.1.call-update
  7.3 0.0 all-gather.6.cloned.1.call-start
  7.3 1.2 dynamic_slice.9
  8.6 0.6 iota_compare_fusion.2
  9.2 0.8 select_reduce_fusion.1
  10.0 0.8 broadcast_compare_fusion
  10.8 0.1 iota_compare_fusion
  10.9 0.0 copy-start.2
  10.9 50.4 %all-gather.4.cloned.1.call-done = bf16[2,8,256,256]{3,2,1,0:T(8,128)(2,1)} async-done(((bf16[2,1,256,256]{3,2,1,0:T(8,128)(2,1)}), bf16[2,8,256,256]{3,2,1,0:T(8,128)(2,1)}) %all-gather.4.cloned.1.call-update) | async-done | bytes 2097168 | tf_op jit(solution)/shard_map/all_gather | solution.py:38
  61.3 4.3 %gather_fusion = bf16[16,2,256,256]{3,2,1,0:T(8,128)(2,1)} fusion(bf16[2,8,256,256]{3,2,1,0:T(8,128)(2,1)} %all-gather.4.cloned.1.call-done, s32[1024]{0:T(1024)S(1)} %pad_clamp_fusion), kind=kCustom, calls=%fused_computation | custom fusion | bytes 8388672 | tf_op jit(solution)/shard_map/jit(_take)/gather | solution.py:39
  65.7 0.0 copy-done.2
  65.7 5.5 %convert_bitcast_fusion.1 = bf16[16,2,256,256]{2,3,1,0:T(8,128)(2,1)} fusion(bf16[16,2,256,256]{3,2,1,0:T(8,128)(2,1)} %gather_fusion, pred[16]{0:T(512)(128)(4,1)S(1)} %compare_and_fusion, bf16[1,16,256,256]{3,2,1,0:T(8,128)(2,1)S(1)} %copy-done.2, pred[16,256]{1,0:T(8,128)(4,1)S(1)} %iota_compare_fusion, pred[256]{0:T(512)(128)(4,1)S(1)} %iota_compare_fusion.2), kind=kOutput, calls=%fused_computation.7 | convolution fusion | flops 1080033280 | bytes 10490128 | tf_op jit(solution)/shard_map/bac,hbxc->bhax/dot_general | solution.py:40
  71.2 0.0 copy-start.1
  71.2 7.9 %copy.18 = bf16[16,2,256,256]{3,0,2,1:T(8,128)(2,1)} copy(bf16[16,2,256,256]{2,3,1,0:T(8,128)(2,1)} %convert_bitcast_fusion.1) | data formatting | bytes 8388608 | tf_op jit(solution)/shard_map/convert_element_type | solution.py:42
  79.1 0.0 copy-done.1
  79.1 3.4 %convert_bitcast_fusion = bf16[16,2,256,256]{3,0,2,1:T(8,128)(2,1)S(1)} fusion(bf16[16,2,256,256]{3,0,2,1:T(8,128)(2,1)} %copy.18, bf16[2,16,16]{2,1,0:T(8,128)(2,1)S(1)} %copy-done.1, pred[16,16]{1,0:T(8,128)(4,1)S(1)} %broadcast_compare_fusion), kind=kOutput, calls=%fused_computation.6 | convolution fusion | flops 69206528 | bytes 8389888 | tf_op jit(solution)/shard_map/nhst,nthac->nshac/dot_general | solution.py:46
  82.5 0.0 copy-done
  82.5 6.1 %fusion.8 = f32[1,16,256,256]{2,3,1,0:T(8,128)} fusion(bf16[16,2,256,256]{3,0,2,1:T(8,128)(2,1)S(1)} %convert_bitcast_fusion, bf16[2,1,256,256]{3,2,1,0:T(8,128)(2,1)S(1)} %copy-done), kind=kOutput, calls=%fused_computation.9 | convolution fusion | flops 1073741824 | bytes 8650752 | tf_op jit(solution)/shard_map/hnab,nshbc->nsac/dot_general | solution.py:49
  88.7 5.3 %copy.20 = f32[1,16,256,256]{3,2,1,0:T(8,128)} copy(f32[1,16,256,256]{2,3,1,0:T(8,128)} %fusion.8) | data formatting | bytes 8388608 | tf_op jit(solution)/shard_map/hnab,nshbc->nsac/transpose | solution.py:49
  94.0 0.0 all-gather.6.cloned.1.call-update
  94.0 0.6 broadcast_and_fusion
  94.7 104.0 %all-gather.6.cloned.1.call-done = f32[4,16,256,256]{3,2,1,0:T(8,128)} async-done(((f32[1,16,256,256]{3,2,1,0:T(8,128)}), f32[4,16,256,256]{3,2,1,0:T(8,128)}) %all-gather.6.cloned.1.call-update) | async-done | bytes 16777232 | tf_op jit(solution)/shard_map/all_gather | solution.py:54
  198.6 7.5 %reduce.3 = bf16[16,256,256]{2,1,0:T(8,128)(2,1)S(1)} reduce(f32[4,16,256,256]{3,2,1,0:T(8,128)} %all-gather.6.cloned.1.call-done, f32[]{:T(128)} %constant.34.clone.1), dimensions={0}, to_apply=%region_2.3 | reduce | flops 3145728 | bytes 18874372 | tf_op jit(solution)/shard_map/reduce_sum | solution.py:55
  206.2 1.0 fusion.14
  (3 shorter events, 0.0 us)
Async XLA Ops:
  6.5 76.0 %copy-start = (bf16[2,1,256,256]{3,2,1,0:T(8,128)(2,1)S(1)}, bf16[2,1,256,256]{3,2,1,0:T(8,128)(2,1)}, u32[]{:S(2)}) copy-start(bf16[2,1,256,256]{3,2,1,0:T(8,128)(2,1)} %param.9) | copy-start | bytes 786436
  6.5 54.8 %all-gather.4.cloned.1.call-start = ((), (), s32[]{:S(2)}) async-start(), calls=%async_computation | async-start | bytes 2359296 | tf_op jit(solution)/shard_map/all_gather | solution.py:38
  7.3 191.4 %all-gather.6.cloned.1.call-start = ((), (), s32[]{:S(2)}) async-start(), calls=%async_computation.1 | async-start | bytes 20971520 | tf_op jit(solution)/shard_map/all_gather | solution.py:54
  10.9 54.8 %copy-start.2 = (bf16[1,16,256,256]{3,2,1,0:T(8,128)(2,1)S(1)}, bf16[1,16,256,256]{3,2,1,0:T(8,128)(2,1)}, u32[]{:S(2)}) copy-start(bf16[1,16,256,256]{3,2,1,0:T(8,128)(2,1)} %param.8) | copy-start | bytes 6291460
  71.2 7.9 %copy-start.1 = (bf16[2,16,16]{2,1,0:T(8,128)(2,1)S(1)}, bf16[2,16,16]{2,1,0:T(8,128)(2,1)}, u32[]{:S(2)}) copy-start(bf16[2,16,16]{2,1,0:T(8,128)(2,1)} %param.11) | copy-start | bytes 3076
Sparse Core Ops, SparseCore 0:
  9.5 51.7 all-gather.3
  94.2 104.4 all-gather.5
